TPU v7x, 32 devices: a whole 2x2x4 slice. The times are simulated.
32 devices in a mesh: gx: 16 (over z, y, core), gy: 2 (over x).
Axes of the slice: x: 2, y: 2, z: 4, core: 2. Of those that a mesh axis runs over, the one named last changes fastest.
Arguments:
- displacement: float32 [3, 128, 32, 512], P(None, 'gx', 'gy'), may hold values from -1.2 to 1.2
- density: float32 [128, 32, 512], P('gx', 'gy'), may hold values from 0.1 to 1
- stiffness: float32 [24, 24], replicated, may hold values from -16 to 17, as said below
Outputs:
- sensitivity: float32 [128, 32, 512], P('gx', 'gy')
- filtered: float32 [128, 32, 512], P('gx', 'gy')
Inputs may be any that keep to these rules, and one draw needn't show every extreme that they name: `stiffness`: symmetric positive definite.
All inputs are finite; a program needn't handle non-finite values.
Results may differ from a plain program's by a relative error of at most 0.00025.
Values sent between devices are 32-bit elements; how exact they have to be, the bound alone decides.
A program may use at most 64 MiB of HBM per device.

v0:
```python
import jax
import jax.numpy as jnp
from jax import lax
from jax.sharding import PartitionSpec as P

ITERS = 3


penal = 3.0
e_min = 0.001
filter_weight = 2.0


def with_halo(cells, sides, width):
    for axis, dim in sides:
        count = lax.axis_size(axis)
        ends = count - 1
        head = lax.slice_in_dim(cells, 0, width, axis=dim)
        tail = lax.slice_in_dim(cells, cells.shape[dim] - width, cells.shape[dim], axis=dim)
        cells = jnp.concatenate(
            [
                lax.ppermute(tail, axis, [(i, (i + 1) % count) for i in range(ends)]),
                cells,
                lax.ppermute(head, axis, [((i + 1) % count, i) for i in range(ends)]),
            ],
            axis=dim,
        )
    return cells


def from_behind(value, axis, steps):
    count = lax.axis_size(axis)
    first, last = (max(0, -steps), min(count, count - steps))
    return lax.ppermute(value, axis, [(source, source + steps) for source in range(first, last)])


def corner_views(block, size_x, size_y, size_z):
    views = []
    for offset_x in (0, 1):
        for offset_y in (0, 1):
            for offset_z in (0, 1):
                for comp in range(3):
                    views.append(
                        block[
                            comp,
                            offset_x : offset_x + size_x,
                            offset_y : offset_y + size_y,
                            offset_z : offset_z + size_z,
                        ]
                    )
    return views


def element_energy(views, stiffness):
    energy = jnp.zeros_like(views[0])
    count = len(views)
    for row_index in range(count):
        weighted = stiffness[row_index, 0] * views[0]
        for col_index in range(1, count):
            weighted = weighted + stiffness[row_index, col_index] * views[col_index]
        energy = energy + views[row_index] * weighted
    return energy


def apply_filter(field, neighbours):
    padded = with_halo(field, (("gx", 0), ("gy", 1)), 1)
    beside = padded[2:, 1:-1] + padded[:-2, 1:-1] + padded[1:-1, 2:] + padded[1:-1, :-2]
    along_z = jnp.pad(field, ((0, 0), (0, 0), (1, 1)))
    beside = beside + along_z[:, :, 2:] + along_z[:, :, :-2]
    return (1.0 + filter_weight * neighbours) * field - filter_weight * beside


def count_neighbours(index_x, index_y, index_z, total_x, total_y, total_z):
    missing = (index_x == 0).astype(jnp.float32) + (index_x == total_x - 1).astype(jnp.float32)
    missing = (
        missing + (index_y == 0).astype(jnp.float32) + (index_y == total_y - 1).astype(jnp.float32)
    )
    missing = (
        missing + (index_z == 0).astype(jnp.float32) + (index_z == total_z - 1).astype(jnp.float32)
    )
    return 6.0 - missing


def global_pair(pair):
    partial_pair = lax.psum((pair[0], pair[1]), "gy")
    return lax.psum((partial_pair[0], partial_pair[1]), "gx")


def conjugate_steps(residual, inverse, operate, owned):
    solution = jnp.zeros_like(residual)
    direction = jnp.zeros_like(residual)
    image_dir = jnp.zeros_like(residual)
    step_old = jnp.float32(1.0)
    dot_old = jnp.float32(1.0)
    for iteration in range(ITERS):
        scaled = inverse * residual
        image = operate(scaled)
        residual_dot, curvature = global_pair(
            (jnp.sum(owned(residual * scaled)), jnp.sum(owned(image * scaled)))
        )
        if iteration == 0:
            step_size = residual_dot / curvature
            direction = scaled
            image_dir = image
        else:
            momentum = residual_dot / dot_old
            step_size = residual_dot / (curvature - momentum * residual_dot / step_old)
            direction = scaled + momentum * direction
            image_dir = image + momentum * image_dir
        solution = solution + step_size * direction
        residual = residual - step_size * image_dir
        step_old = step_size
        dot_old = residual_dot
    return solution


def per_device(displacement, density, stiffness):
    comps, size_x, size_y, size_z = displacement.shape
    upper_x = from_behind(displacement[:, :1], "gx", -1)
    widened = jnp.concatenate([displacement, upper_x], axis=1)
    upper_y = from_behind(widened[:, :, :1], "gy", -1)
    extended = jnp.concatenate([widened, upper_y], axis=2)
    extended = jnp.pad(extended, ((0, 0), (0, 0), (0, 0), (0, 1)))
    views = corner_views(extended, size_x, size_y, size_z)
    energy = element_energy(views, stiffness)
    sensitivity = -penal * density * density * (1.0 - e_min) * energy
    total_x = size_x * lax.axis_size("gx")
    total_y = size_y * lax.axis_size("gy")
    index_z = jnp.arange(size_z, dtype=jnp.int32)[None, None, :]
    index_x = lax.axis_index("gx") * size_x + jnp.arange(size_x, dtype=jnp.int32)[:, None, None]
    index_y = lax.axis_index("gy") * size_y + jnp.arange(size_y, dtype=jnp.int32)[None, :, None]
    neighbours = count_neighbours(index_x, index_y, index_z, total_x, total_y, size_z)
    inverse = 1.0 / (1.0 + filter_weight * neighbours)

    def operate_here(field):
        return apply_filter(field, neighbours)

    def whole_block(values):
        return values

    solution = conjugate_steps(sensitivity, inverse, operate_here, whole_block)
    return (sensitivity, solution)


def solution(mesh):
    placed = (P(None, "gx", "gy", None), P("gx", "gy", None), P())
    return jax.shard_map(
        per_device,
        mesh=mesh,
        in_specs=placed,
        out_specs=(P("gx", "gy", None), P("gx", "gy", None)),
        check_vma=False,
    )
```

profile of v0, /device:TPU:0, one launch (start us, length us, event | category | flops | bytes accessed | tf_op | source)
XLA Modules:
  0.0 573.5 jit_solution(5537071258607539355)
XLA Ops:
  0.6 0.9 slice.1936
  1.5 1.3 collective-permute-start
  2.8 2.1 fusion.678
  4.9 2.1 fusion.677
  7.0 1.2 constant_dynamic-update-slice_fusion.1
  8.2 0.7 fusion.682
  9.0 0.7 fusion.687
  9.7 0.7 fusion.684
  10.4 0.7 fusion.683
  11.2 0.7 fusion.689
  11.9 0.7 fusion.690
  12.6 0.7 fusion.691
  13.4 0.7 fusion.692
  14.1 0.7 fusion.685
  17.0 0.7 fusion.680
  19.9 0.7 fusion.672
  20.6 0.7 fusion.671
  21.4 0.7 fusion.670
  23.5 0.7 fusion.675
  26.4 0.7 fusion.667
  27.1 0.7 fusion.694
  28.6 0.7 fusion.696
  30.2 1.3 collective-permute-start.1
  31.5 5.9 %broadcast_multiply_fusion.199 = (f32[8,16,512]{2,1,0:T(8,128)S(1)}, f32[8,16,512]{2,1,0:T(8,128)S(1)}, f32[8,16,512]{2,1,0:T(8,128)S(1)}, f32[8,16,512]{2,1,0:T...) fusion(f32[]{:T(128)} %bitcast.252, ...), kind=kLoop, calls=%fused_computation.991 | loop fusion | flops 589824 | bytes 2621476 | tf_op jit(solution)/shard_map/mul | solution.py:60
  37.4 4.0 broadcast_multiply_fusion.205
  41.4 5.9 %broadcast_multiply_fusion.172 = (f32[8,16,512]{2,1,0:T(8,128)S(1)}, f32[8,16,512]{2,1,0:T(8,128)S(1)}, f32[8,16,512]{2,1,0:T(8,128)S(1)}, f32[8,16,512]{2,1,0:T...) fusion(f32[8,16,512]{2,1,0:T(8,128)S(1)} %get-tuple-element.52,, ...), kind=kLoop, calls=%fused_computation.964 | loop fusion | flops 589824 | bytes 2621476 | tf_op jit(solution)/shard_map/mul | solution.py:60
  47.3 5.8 %broadcast_multiply_fusion.182 = (f32[8,16,512]{2,1,0:T(8,128)S(1)}, f32[8,16,512]{2,1,0:T(8,128)S(1)}, f32[8,16,512]{2,1,0:T(8,128)S(1)}, f32[8,16,512]{2,1,0:T...) fusion(f32[8,16,512]{2,1,0:T(8,128)S(1)} %get-tuple-element.50,, ...), kind=kLoop, calls=%fused_computation.974 | loop fusion | flops 589824 | bytes 2621476 | tf_op jit(solution)/shard_map/mul | solution.py:60
  53.0 6.0 %broadcast_multiply_fusion.171 = (f32[8,16,512]{2,1,0:T(8,128)S(1)}, f32[8,16,512]{2,1,0:T(8,128)S(1)}, f32[8,16,512]{2,1,0:T(8,128)S(1)}, f32[8,16,512]{2,1,0:T...) fusion(f32[8,16,512]{2,1,0:T(8,128)S(1)} %get-tuple-element.54,, ...), kind=kLoop, calls=%fused_computation.963 | loop fusion | flops 589824 | bytes 2621476 | tf_op jit(solution)/shard_map/mul | solution.py:60
  59.1 6.0 %broadcast_multiply_fusion.170 = (f32[8,16,512]{2,1,0:T(8,128)S(1)}, f32[8,16,512]{2,1,0:T(8,128)S(1)}, f32[8,16,512]{2,1,0:T(8,128)S(1)}, f32[8,16,512]{2,1,0:T...) fusion(f32[8,16,512]{2,1,0:T(8,128)S(1)} %get-tuple-element.56,, ...), kind=kLoop, calls=%fused_computation.962 | loop fusion | flops 589824 | bytes 2621476 | tf_op jit(solution)/shard_map/mul | solution.py:60
  65.1 5.9 %broadcast_multiply_fusion.184 = (f32[8,16,512]{2,1,0:T(8,128)S(1)}, f32[8,16,512]{2,1,0:T(8,128)S(1)}, f32[8,16,512]{2,1,0:T(8,128)S(1)}, f32[8,16,512]{2,1,0:T...) fusion(f32[8,16,512]{2,1,0:T(8,128)S(1)} %get-tuple-element.27,, ...), kind=kLoop, calls=%fused_computation.976 | loop fusion | flops 589824 | bytes 2621476 | tf_op jit(solution)/shard_map/mul | solution.py:60
  71.0 5.9 %broadcast_multiply_fusion.183 = (f32[8,16,512]{2,1,0:T(8,128)S(1)}, f32[8,16,512]{2,1,0:T(8,128)S(1)}, f32[8,16,512]{2,1,0:T(8,128)S(1)}, f32[8,16,512]{2,1,0:T...) fusion(f32[8,16,512]{2,1,0:T(8,128)S(1)} %get-tuple-element.48,, ...), kind=kLoop, calls=%fused_computation.975 | loop fusion | flops 589824 | bytes 2621476 | tf_op jit(solution)/shard_map/mul | solution.py:60
  77.0 6.2 %broadcast_multiply_fusion.188 = (f32[8,16,512]{2,1,0:T(8,128)S(1)}, f32[8,16,512]{2,1,0:T(8,128)S(1)}, f32[8,16,512]{2,1,0:T(8,128)S(1)}, f32[8,16,512]{2,1,0:T...) fusion(f32[]{:T(128)} %bitcast.263, ...), kind=kLoop, calls=%fused_computation.980 | loop fusion | flops 589824 | bytes 3299364 | tf_op jit(solution)/shard_map/mul | solution.py:60
  83.3 1.1 copy-done
  84.4 139.8 %fusion.239 = f32[8,16,512]{2,1,0:T(8,128)S(1)} fusion(f32[8,16,512]{2,1,0:T(8,128)S(1)} %get-tuple-element.48, f32[8,16,512]{2,1,0:T(8,128)S(1)} %get-tuple-element.50, f32[8,16,512]{2,1,0:T(8,128)S(1)} %get-tuple-element.27, f32[8,16,512]{2,1,0:T(8,128)S(1)} %get-tuple-element.56, f32[8,16,512]{2,1,0:T(8,128)S(1)} %get-tuple-element.54, ...), kind=kLoop, calls=%fused_computation.323 | loop fusion | flops 28835840 | bytes 4348768 | tf_op jit(solution)/shard_map/add | solution.py:61
  224.2 107.4 %fusion.479 = f32[8,16,512]{2,1,0:T(8,128)S(1)} fusion(f32[8,16,512]{2,1,0:T(8,128)S(1)} %get-tuple-element.46, f32[8,16,512]{2,1,0:T(8,128)S(1)} %get-tuple-element.126, f32[8,16,512]{2,1,0:T(8,128)S(1)} %get-tuple-element.117, f32[8,16,512]{2,1,0:T(8,128)S(1)} %get-tuple-element.109, f32[8,16,512]{2,1,0:T(8,128)S(1)} %get-tuple-element.60, ...), kind=kLoop, calls=%fused_computation.563 | loop fusion | flops 27000832 | bytes 23747208 | tf_op jit(solution)/shard_map/add | solution.py:61
  331.7 78.1 %fusion.650 = (f32[8,16,512]{2,1,0:T(8,128)S(1)}, f32[8,16,512]{2,1,0:T(8,128)S(1)}) fusion(f32[512]{0:T(512)S(1)} %get-tuple-element.711, f32[512]{0:T(512)S(1)} %get-tuple-element.710, f32[8,16]{1,0:T(8,128)S(1)} %add_add_fusion, f32[]{:T(128)} %bitcast.599, f32[]{:T(128)} %bitcast.598, f32[]{:T(128)} %bitcast.597, ...), kind=kLoop, calls=%fused_computation.791 | loop fusion | flops 16777216 | bytes 5139424 | tf_op jit(solution)/shard_map/mul | solution.py:96
  409.9 1.3 collective-permute-start.2
  411.2 3.7 collective-permute-start.3
  414.9 0.8 collective-permute-done.3
  415.7 1.3 collective-permute-start.4
  417.0 4.8 collective-permute-start.5
  421.9 1.5 collective-permute-done.5
  423.3 0.9 multiply_reduce_fusion.3
  424.2 5.8 %all-reduce.9 = (f32[]{:T(128)}, f32[]{:T(128)}) all-reduce(f32[]{:T(128)} %get-tuple-element.3, f32[]{:T(128)} %get-tuple-element.2), channel_id=1, replica_groups=mesh['gx'=16,'gy'=2] {'gy'}, use_global_device_ids=true, to_apply=%region_1.2 | all-reduce | flops 2 | bytes 16 | tf_op jit(solution)/shard_map/psum | solution.py:85
  430.1 33.7 %all-reduce.6 = (f32[]{:T(128)}, f32[]{:T(128)}) all-reduce(f32[]{:T(128)} %get-tuple-element.18, f32[]{:T(128)} %get-tuple-element.19), channel_id=1, replica_groups=mesh['gx'=16,'gy'=2] {'gx'}, use_global_device_ids=true, to_apply=%region_2.3 | all-reduce | flops 2 | bytes 16 | tf_op jit(solution)/shard_map/psum | solution.py:86
  465.2 1.3 collective-permute-start.6
  466.5 3.0 collective-permute-start.7
  469.6 0.8 collective-permute-done.7
  470.5 1.3 collective-permute-start.8
  471.8 4.5 collective-permute-start.9
  476.3 1.5 collective-permute-done.9
  477.8 0.9 multiply_reduce_fusion.1
  478.7 5.9 %all-reduce.8 = (f32[]{:T(128)}, f32[]{:T(128)}) all-reduce(f32[]{:T(128)} %get-tuple-element.5, f32[]{:T(128)} %get-tuple-element.4), channel_id=1, replica_groups=mesh['gx'=16,'gy'=2] {'gy'}, use_global_device_ids=true, to_apply=%region_7.8 | all-reduce | flops 2 | bytes 16 | tf_op jit(solution)/shard_map/psum | solution.py:85
  484.6 30.1 %all-reduce.5 = (f32[]{:T(128)}, f32[]{:T(128)}) all-reduce(f32[]{:T(128)} %get-tuple-element.16, f32[]{:T(128)} %get-tuple-element.17), channel_id=1, replica_groups=mesh['gx'=16,'gy'=2] {'gx'}, use_global_device_ids=true, to_apply=%region_8.9 | all-reduce | flops 2 | bytes 16 | tf_op jit(solution)/shard_map/psum | solution.py:86
  519.2 1.3 collective-permute-start.10
  520.5 3.0 collective-permute-start.11
  523.5 0.8 collective-permute-done.11
  524.4 1.3 collective-permute-start.12
  525.7 4.5 collective-permute-start.13
  530.3 1.5 collective-permute-done.13
  531.7 0.9 fusion.13
  532.6 6.0 %all-reduce.7 = (f32[]{:T(128)}, f32[]{:T(128)}) all-reduce(f32[]{:T(128)} %get-tuple-element.7, f32[]{:T(128)} %get-tuple-element.6), channel_id=1, replica_groups=mesh['gx'=16,'gy'=2] {'gy'}, use_global_device_ids=true, to_apply=%region_13.14 | all-reduce | flops 2 | bytes 16 | tf_op jit(solution)/shard_map/psum | solution.py:85
  538.6 30.1 %all-reduce.4 = (f32[]{:T(128)}, f32[]{:T(128)}) all-reduce(f32[]{:T(128)} %get-tuple-element.14, f32[]{:T(128)} %get-tuple-element.15), channel_id=1, replica_groups=mesh['gx'=16,'gy'=2] {'gx'}, use_global_device_ids=true, to_apply=%region_14.15 | all-reduce | flops 2 | bytes 16 | tf_op jit(solution)/shard_map/psum | solution.py:86
  572.6 0.9 multiply_add_fusion
  (43 shorter events, 10.0 us)
Async XLA Ops:
  0.6 7.6 %copy-start.2 = (f32[24,24]{1,0:T(8,128)S(1)}, f32[24,24]{1,0:T(8,128)}, u32[]{:S(2)}) copy-start(f32[24,24]{1,0:T(8,128)} %param.5) | copy-start | bytes 6916
  1.5 28.6 %collective-permute-start = (f32[3,1,16,512]{3,2,1,0:T(8,128)S(1)}, f32[3,1,16,512]{3,2,1,0:T(8,128)S(1)}, u32[]{:S(2)}, u32[]{:S(2)}) collective-permute-start(f32[3,1,16,512]{3,2,1,0:T(8,128)S(1)} %slice.1936), channel_id=1, source_target_pairs={{2,0},{4,2},{6,4},{8,6},{10,8},{12,10},{14,12},{16,14},{18,16},{20... | collective-permute-start | bytes 294920 | tf_op jit(solution)/shard_map/ppermute | solution.py:34
  30.2 7.2 %collective-permute-start.1 = (f32[3,9,1,512]{3,2,1,0:T(1,128)S(1)}, f32[3,9,1,512]{3,2,1,0:T(1,128)S(1)}, u32[]{:S(2)}, u32[]{:S(2)}) collective-permute-start(f32[3,9,1,512]{3,2,1,0:T(1,128)S(1)} %slice.2561), channel_id=1, source_target_pairs={{1,0},{3,2},{5,4},{7,6},{9,8},{11,10},{13,12},{15,14},{17,16},{19,... | collective-permute-start | bytes 165896 | tf_op jit(solution)/shard_map/ppermute | solution.py:34
  83.3 1.1 copy-start
  224.2 107.5 %copy-start.3 = (f32[8,16,512]{2,1,0:T(8,128)S(1)}, f32[8,16,512]{2,1,0:T(8,128)}, u32[]{:S(2)}) copy-start(f32[8,16,512]{2,1,0:T(8,128)} %param.4) | copy-start | bytes 786436
  409.8 162.7 %copy-start.1 = (f32[8,16,512]{2,1,0:T(8,128)}, f32[8,16,512]{2,1,0:T(8,128)S(1)}, u32[]{:S(2)}) copy-start(f32[8,16,512]{2,1,0:T(8,128)S(1)} %get-tuple-element.25) | copy-start | bytes 786436
  409.9 5.0 collective-permute-start.2
  411.2 4.5 collective-permute-start.3
  415.7 6.2 %collective-permute-start.4 = (f32[10,1,512]{2,1,0:T(1,128)S(1)}, f32[10,1,512]{2,1,0:T(1,128)S(1)}, u32[]{:S(2)}, u32[]{:S(2)}) collective-permute-start(f32[10,1,512]{2,1,0:T(1,128)S(1)} %get-tuple-element.70), channel_id=1, source_target_pairs={{1,0},{3,2},{5,4},{7,6},{9,8},{11,10},{13,12},{15,14},{17,16},{19,... | collective-permute-start | bytes 61448 | tf_op jit(solution)/shard_map/ppermute | solution.py:24
  417.0 6.3 %collective-permute-start.5 = (f32[10,1,512]{2,1,0:T(1,128)S(1)}, f32[10,1,512]{2,1,0:T(1,128)S(1)}, u32[]{:S(2)}, u32[]{:S(2)}) collective-permute-start(f32[10,1,512]{2,1,0:T(1,128)S(1)} %get-tuple-element.71), channel_id=1, source_target_pairs={{0,1},{2,3},{4,5},{6,7},{8,9},{10,11},{12,13},{14,15},{16,17},{18,... | collective-permute-start | bytes 61448 | tf_op jit(solution)/shard_map/ppermute | solution.py:22
  465.2 4.3 collective-permute-start.6
  466.5 3.9 collective-permute-start.7
  470.5 5.9 %collective-permute-start.8 = (f32[10,1,512]{2,1,0:T(1,128)S(1)}, f32[10,1,512]{2,1,0:T(1,128)S(1)}, u32[]{:S(2)}, u32[]{:S(2)}) collective-permute-start(f32[10,1,512]{2,1,0:T(1,128)S(1)} %get-tuple-element.68), channel_id=1, source_target_pairs={{1,0},{3,2},{5,4},{7,6},{9,8},{11,10},{13,12},{15,14},{17,16},{19,... | collective-permute-start | bytes 61448 | tf_op jit(solution)/shard_map/ppermute | solution.py:24
  471.8 6.0 %collective-permute-start.9 = (f32[10,1,512]{2,1,0:T(1,128)S(1)}, f32[10,1,512]{2,1,0:T(1,128)S(1)}, u32[]{:S(2)}, u32[]{:S(2)}) collective-permute-start(f32[10,1,512]{2,1,0:T(1,128)S(1)} %get-tuple-element.69), channel_id=1, source_target_pairs={{0,1},{2,3},{4,5},{6,7},{8,9},{10,11},{12,13},{14,15},{16,17},{18,... | collective-permute-start | bytes 61448 | tf_op jit(solution)/shard_map/ppermute | solution.py:22
  519.2 4.3 collective-permute-start.10
  520.5 3.9 collective-permute-start.11
  524.4 5.9 %collective-permute-start.12 = (f32[10,1,512]{2,1,0:T(1,128)S(1)}, f32[10,1,512]{2,1,0:T(1,128)S(1)}, u32[]{:S(2)}, u32[]{:S(2)}) collective-permute-start(f32[10,1,512]{2,1,0:T(1,128)S(1)} %get-tuple-element.66), channel_id=1, source_target_pairs={{1,0},{3,2},{5,4},{7,6},{9,8},{11,10},{13,12},{15,14},{17,16},{19,... | collective-permute-start | bytes 61448 | tf_op jit(solution)/shard_map/ppermute | solution.py:24
  525.7 6.0 %collective-permute-start.13 = (f32[10,1,512]{2,1,0:T(1,128)S(1)}, f32[10,1,512]{2,1,0:T(1,128)S(1)}, u32[]{:S(2)}, u32[]{:S(2)}) collective-permute-start(f32[10,1,512]{2,1,0:T(1,128)S(1)} %get-tuple-element.67), channel_id=1, source_target_pairs={{0,1},{2,3},{4,5},{6,7},{8,9},{10,11},{12,13},{14,15},{16,17},{18,... | collective-permute-start | bytes 61448 | tf_op jit(solution)/shard_map/ppermute | solution.py:22
where the time goes:
time: 579 us; the launch traced here: 573 us
  other arithmetic  381 us (66%)
  blocking collectives  112 us (19%)
  starting transfers between devices  34 us (6%)
  local copies, waits for them, and re-layouts  29.2 us (5%)
  between operations  10.5 us (2%)
  waiting for transfers between devices  6.87 us (1%)
    add x2, other arithmetic, element_energy(): energy = energy + views[row_index] * weighted  247 us
    psum x3, blocking collectives, global_pair(): return lax.psum((partial_pair[0], partial_pair[1]), 'gx')  94 us
    mul x3, other arithmetic, conjugate_steps(): scaled = inverse * residual  78.4 us
    mul x9, other arithmetic, element_energy(): weighted = weighted + stiffness[row_index, col_index] * views[col_index]  51.6 us
    slice x30, local copies, waits for them, and re-layouts, element_energy(): weighted = weighted + stiffness[row_index, col_index] * views[col_index]  24.5 us
    ppermute x6, starting transfers between devices, with_halo(): lax.ppermute(tail, axis, [(i, (i + 1) % count) for i in range(ends)])  23.7 us
    psum x3, blocking collectives, global_pair(): partial_pair = lax.psum((pair[0], pair[1]), 'gy')  17.7 us
  transfers between devices with their start and end apart: 14, of which 6 were waited for; matrix products, arithmetic and copies ran while one was open for 6% of the time, Pallas kernels for 0%

commit v1 on v0

v1 whole, which is shorter than its diff:
```python
import functools

import jax
import jax.numpy as jnp
from jax import lax
from jax.experimental import pallas as pl
from jax.experimental.pallas import tpu as pltpu
from jax.sharding import PartitionSpec as P

MESH = pl.DeviceIdType.MESH
penal = 3.0
e_min = 0.001
filter_weight = 2.0


def kernel(
    n_x, n_y,
    disp, dens, stiff,
    sens, filt,
    views, x_in, y_out, y_in, c_out, c_in,
    field0, field1, field2, image0, image1, image2, face_out, face_in, dots_out, dots_in,
    halo_send, halo_recv, face_send, face_recv, dots_send, dots_recv,
):
    size_x, size_y, size_z = dens.shape
    me_x, me_y = lax.axis_index("gx"), lax.axis_index("gy")
    me = me_x * n_y + me_y
    count = n_x * n_y
    has_xp, has_xn = me_x > 0, me_x < n_x - 1
    has_yp, has_yn = me_y > 0, me_y < n_y - 1

    def place(index):
        return {"gx": index // n_y, "gy": lax.rem(index, n_y)}

    barrier = pltpu.get_barrier_semaphore()

    @pl.loop(1, count)
    def _(offset):
        pl.semaphore_signal(
            barrier, inc=1, device_id=place(lax.rem(me + offset, count)), device_id_type=MESH
        )

    c_out[...] = jnp.zeros_like(c_out)
    for m in range(3):
        for i in range(size_x):
            y_out[m, i : i + 1, :] = disp[m, i, 0:1, :]
        c_out[m : m + 1, :] = disp[m, 0, 0:1, :]

    @pl.when(jnp.logical_not(has_xn))
    def _():
        x_in[...] = jnp.zeros_like(x_in)
        for field in (field0, field1, field2):
            field[size_x + 1] = jnp.zeros((size_y, size_z), jnp.float32)

    @pl.when(jnp.logical_not(has_xp))
    def _():
        for field in (field0, field1, field2):
            field[0] = jnp.zeros((size_y, size_z), jnp.float32)

    @pl.when(jnp.logical_not(has_yn))
    def _():
        y_in[...] = jnp.zeros_like(y_in)
        for step in range(3):
            face_in[step, 1] = jnp.zeros((size_x, size_z), jnp.float32)

    @pl.when(jnp.logical_not(has_yp))
    def _():
        for step in range(3):
            face_in[step, 0] = jnp.zeros((size_x, size_z), jnp.float32)

    @pl.when(jnp.logical_not(jnp.logical_and(has_xn, has_yn)))
    def _():
        c_in[...] = jnp.zeros_like(c_in)

    pl.semaphore_wait(barrier, count - 1)

    def remote(src, dst, send, recv, to_x, to_y):
        return pltpu.make_async_remote_copy(
            src_ref=src, dst_ref=dst, send_sem=send, recv_sem=recv,
            device_id={"gx": to_x, "gy": to_y}, device_id_type=MESH,
        )

    halo_x = remote(disp.at[:, 0], x_in, halo_send.at[0], halo_recv.at[0], me_x - 1, me_y)
    halo_y = remote(y_out, y_in, halo_send.at[1], halo_recv.at[1], me_x, me_y - 1)
    halo_c = remote(c_out, c_in, halo_send.at[2], halo_recv.at[2], me_x - 1, me_y - 1)
    halos = (
        (halo_x, has_xp, has_xn),
        (halo_y, has_yp, has_yn),
        (halo_c, jnp.logical_and(has_xp, has_yp), jnp.logical_and(has_xn, has_yn)),
    )
    for copy, sends, _ in halos:
        pl.when(sends)(copy.start)

    rows = lax.broadcasted_iota(jnp.int32, (size_y, size_z), 0)
    lanes = lax.broadcasted_iota(jnp.int32, (size_y, size_z), 1)

    def later_z(value):
        return jnp.where(lanes == size_z - 1, 0.0, pltpu.roll(value, size_z - 1, 1))

    def earlier_z(value):
        return jnp.where(lanes == 0, 0.0, pltpu.roll(value, 1, 1))

    def put_views(m, i, value, last_row):
        upper = pltpu.roll(value, size_y - 1, 0)
        if last_row is not None:
            upper = jnp.where(rows == size_y - 1, jnp.broadcast_to(last_row, value.shape), upper)
        views[0, m, i] = value
        views[1, m, i] = later_z(value)
        views[2, m, i] = upper
        views[3, m, i] = later_z(upper)

    @pl.loop(0, size_x)
    def _(i):
        for m in range(3):
            put_views(m, i, disp[m, i], None)

    def energy_block(i, start):
        def view(dof):
            a, b, c, m = dof // 12, dof // 6 % 2, dof // 3 % 2, dof % 3
            return views[2 * b + c, m, i + a, start : start + 8, :]

        energy = None
        for row in range(24):
            weighted = (0.5 * stiff[row, row]) * view(row)
            for col in range(row + 1, 24):
                weighted = weighted + stiff[row, col] * view(col)
            term = view(row) * weighted
            energy = term if energy is None else energy + term
        rho = dens[i, start : start + 8, :]
        sens[i, start : start + 8, :] = (-2.0 * penal * (1.0 - e_min)) * (rho * rho) * energy

    @pl.loop(0, size_x - 1)
    def _(i):
        energy_block(i, 0)

    for copy, sends, receives in halos:
        pl.when(receives)(copy.wait_recv)
    for m in range(3):
        put_views(m, size_x, x_in[m], c_in[m : m + 1, :])

    @pl.loop(0, size_x)
    def _(i):
        for m in range(3):
            last = y_in[m, pl.ds(i, 1), :]
            views[2, m, i, size_y - 1 : size_y, :] = last
            views[3, m, i, size_y - 1 : size_y, :] = jnp.where(
                lanes[:1] == size_z - 1, 0.0, pltpu.roll(last, size_z - 1, 1)
            )

    for start in range(8, size_y, 8):
        @pl.loop(0, size_x)
        def _(i):
            energy_block(i, start)

    energy_block(size_x - 1, 0)

    for copy, sends, _ in halos:
        pl.when(sends)(copy.wait_send)

    plane = 6.0 - (lanes == 0).astype(jnp.float32) - (lanes == size_z - 1).astype(jnp.float32)
    row_low = jnp.logical_and(rows == 0, jnp.logical_not(has_yp))
    row_high = jnp.logical_and(rows == size_y - 1, jnp.logical_not(has_yn))
    plane = plane - row_low.astype(jnp.float32) - row_high.astype(jnp.float32)

    def diagonal(i):
        at_low = jnp.logical_and(i == 0, jnp.logical_not(has_xp))
        at_high = jnp.logical_and(i == size_x - 1, jnp.logical_not(has_xn))
        missing = at_low.astype(jnp.float32) + at_high.astype(jnp.float32)
        return 1.0 + filter_weight * (plane - missing)

    def put_field(step, field, i, value):
        field[i + 1] = value
        face_out[step, 0, pl.ds(i, 1), :] = value[0:1]
        face_out[step, 1, pl.ds(i, 1), :] = value[size_y - 1 : size_y]

    def faces(step, field):
        return (
            (remote(field.at[1], field.at[size_x + 1], face_send.at[step, 0],
                    face_recv.at[step, 0], me_x - 1, me_y), has_xp, has_xn),
            (remote(field.at[size_x], field.at[0], face_send.at[step, 1],
                    face_recv.at[step, 1], me_x + 1, me_y), has_xn, has_xp),
            (remote(face_out.at[step, 0], face_in.at[step, 1], face_send.at[step, 2],
                    face_recv.at[step, 2], me_x, me_y - 1), has_yp, has_yn),
            (remote(face_out.at[step, 1], face_in.at[step, 0], face_send.at[step, 3],
                    face_recv.at[step, 3], me_x, me_y + 1), has_yn, has_yp),
        )

    def exchange(step, field):
        copies = faces(step, field)
        for copy, sends, _ in copies:
            pl.when(sends)(copy.start)
        for copy, _, receives in copies:
            pl.when(receives)(copy.wait_recv)
        return copies

    def apply(step, field, i):
        value = field[i + 1]
        below = jnp.where(rows == 0, jnp.broadcast_to(face_in[step, 0, pl.ds(i, 1), :], value.shape),
                          pltpu.roll(value, 1, 0))
        above = jnp.where(rows == size_y - 1,
                          jnp.broadcast_to(face_in[step, 1, pl.ds(i, 1), :], value.shape),
                          pltpu.roll(value, size_y - 1, 0))
        beside = field[i] + field[i + 2] + below + above + later_z(value) + earlier_z(value)
        return diagonal(i) * value - filter_weight * beside

    def fold(value):
        part = value[0:8]
        for start in range(8, size_y, 8):
            part = part + value[start : start + 8]
        total = part[:, 0:128]
        for start in range(128, size_z, 128):
            total = total + part[:, start : start + 128]
        return total

    tile_row = lax.broadcasted_iota(jnp.int32, (8, 128), 0)
    tile_lane = lax.broadcasted_iota(jnp.int32, (8, 128), 1)

    def send_dots(which, parts):
        packed = jnp.zeros((8, 128), jnp.float32)
        for index, part in enumerate(parts):
            packed = packed + jnp.where(
                tile_row == index, jnp.broadcast_to(jnp.sum(part, axis=0, keepdims=True), (8, 128)), 0.0
            )
        totals = jnp.broadcast_to(jnp.sum(packed, axis=1, keepdims=True), (8, 128))
        row = jnp.sum(jnp.where(tile_row == tile_lane, totals, 0.0), axis=0, keepdims=True)
        dots_out[which] = row
        dots_in[which, count - 1] = row

        @pl.loop(1, count)
        def _(offset):
            to = place(lax.rem(me + offset, count))
            remote(dots_out.at[which], dots_in.at[which, offset - 1], dots_send.at[which],
                   dots_recv.at[which], to["gx"], to["gy"]).start()

    def take_dots(which, number):
        whole = dots_in.at[which, pl.ds(0, count - 1)]
        pltpu.make_async_copy(whole, whole, dots_recv.at[which]).wait()
        row = jnp.sum(dots_in[which], axis=0)
        return [
            jnp.sum(jnp.where(tile_lane[:1] == index, row, 0.0), axis=1, keepdims=True)
            for index in range(number)
        ]

    @pl.loop(0, size_x)
    def _(i):
        put_field(0, field0, i, sens[i] / diagonal(i))

    zero = jnp.zeros((8, 128), jnp.float32)
    sent = exchange(0, field0)

    def first(i, sums):
        image = apply(0, field0, i)
        image0[i] = image
        put_field(1, field1, i, image / diagonal(i))
        scaled = field0[i + 1]
        return (sums[0] + fold(sens[i] * scaled), sums[1] + fold(image * scaled))

    dots = lax.fori_loop(0, size_x, first, (zero, zero))
    send_dots(0, dots)
    sent = sent + exchange(1, field1)

    @pl.loop(0, size_x)
    def _(i):
        image = apply(1, field1, i)
        image1[i] = image
        put_field(2, field2, i, image / diagonal(i))

    sent = sent + exchange(2, field2)

    @pl.loop(0, size_x)
    def _(i):
        image2[i] = apply(2, field2, i)

    g0, k0 = take_dots(0, 2)
    s0 = g0 / k0

    def second(i, sums):
        w1, im0, im1 = field1[i + 1], image0[i], image1[i]
        z1 = field0[i + 1] - s0 * w1
        r1 = sens[i] - s0 * im0
        az1 = im0 - s0 * im1
        y1 = w1 - s0 * field2[i + 1]
        ay1 = im1 - s0 * image2[i]
        terms = (r1 * z1, z1 * az1, y1 * az1, az1 * w1, w1 * im0, y1 * ay1, y1 * im1, w1 * im1)
        return tuple(total + fold(term) for total, term in zip(sums, terms))

    dots = lax.fori_loop(0, size_x, second, (zero,) * 8)
    send_dots(1, dots)
    g1, c1, d1, d2, d3, e1, e2, e3 = take_dots(1, 8)
    b1 = g1 / g0
    s1 = g1 / (c1 - b1 * g1 / s0)
    d0 = -g1 / s0
    g2 = g1 - 2.0 * s1 * (c1 + b1 * d0) + s1 * s1 * (d1 + 2.0 * b1 * d2 + b1 * b1 * d3)
    g2 = jnp.maximum(g2, 0.0)
    c2 = c1 - 2.0 * s1 * (d1 + b1 * d2) + s1 * s1 * (e1 + 2.0 * b1 * e2 + b1 * b1 * e3)
    b2 = g2 / g1
    s2 = g2 / (c2 - b2 * g2 / s1)
    t1 = s0 + s1 * (1.0 + b1)
    weight0 = t1 + s2 * (1.0 + b2 * (1.0 + b1))
    weight1 = -(s1 * s0 + s2 * (t1 + b2 * s0))
    weight2 = s2 * s0 * s1

    @pl.loop(0, size_x)
    def _(i):
        filt[i] = weight0 * field0[i + 1] + weight1 * field1[i + 1] + weight2 * field2[i + 1]

    for copy, sends, _ in sent:
        pl.when(sends)(copy.wait_send)
    for which in range(2):
        whole = dots_in.at[which, pl.ds(0, count - 1)]
        pltpu.make_async_copy(whole, whole, dots_send.at[which]).wait()


def solution(mesh):
    n_x, n_y = mesh.shape["gx"], mesh.shape["gy"]

    def per_device(displacement, density, stiffness):
        size_x, size_y, size_z = density.shape
        block = (size_x, size_y, size_z)
        wide = pltpu.VMEM((size_x + 2, size_y, size_z), jnp.float32)
        same = pltpu.VMEM(block, jnp.float32)
        vmem = pl.BlockSpec(memory_space=pltpu.VMEM)
        return pl.pallas_call(
            functools.partial(kernel, n_x, n_y),
            out_shape=(jax.ShapeDtypeStruct(block, jnp.float32),) * 2,
            in_specs=[vmem, vmem, pl.BlockSpec(memory_space=pltpu.SMEM)],
            out_specs=(vmem, vmem),
            scratch_shapes=[
                pltpu.VMEM((4, 3, size_x + 1, size_y, size_z), jnp.float32),
                pltpu.VMEM((3, size_y, size_z), jnp.float32),
                pltpu.VMEM((3, size_x, size_z), jnp.float32),
                pltpu.VMEM((3, size_x, size_z), jnp.float32),
                pltpu.VMEM((8, size_z), jnp.float32),
                pltpu.VMEM((8, size_z), jnp.float32),
                wide, wide, wide, same, same, same,
                pltpu.VMEM((3, 2, size_x, size_z), jnp.float32),
                pltpu.VMEM((3, 2, size_x, size_z), jnp.float32),
                pltpu.VMEM((2, 1, 128), jnp.float32),
                pltpu.VMEM((2, n_x * n_y, 1, 128), jnp.float32),
                pltpu.SemaphoreType.DMA((3,)),
                pltpu.SemaphoreType.DMA((3,)),
                pltpu.SemaphoreType.DMA((3, 4)),
                pltpu.SemaphoreType.DMA((3, 4)),
                pltpu.SemaphoreType.DMA((2,)),
                pltpu.SemaphoreType.DMA((2,)),
            ],
            compiler_params=pltpu.CompilerParams(
                collective_id=0, has_side_effects=True, vmem_limit_bytes=48 * 1024 * 1024
            ),
        )(displacement, density, stiffness)

    return jax.shard_map(
        per_device,
        mesh=mesh,
        in_specs=(P(None, "gx", "gy", None), P("gx", "gy", None), P()),
        out_specs=(P("gx", "gy", None), P("gx", "gy", None)),
        check_vma=False,
    )
```

time: 579 us -> 37.3 us (0.06)
  other arithmetic: 381 us -> 0 us
  blocking collectives: 112 us -> 0 us
  starting transfers between devices: 34 us -> 0 us
  Pallas kernels: 0 us -> 32.2 us
  local copies, waits for them, and re-layouts: 29.2 us -> 4.19 us
  between operations: 10.5 us -> 0.65 us
  waiting for transfers between devices: 6.87 us -> 0 us
    add x5 -> x0, other arithmetic: 248 us -> none  [the longest x2 247 us: element_energy(): energy = energy + views[row_index] * weighted]
    mul x12 -> x0, other arithmetic: 130 us -> none  [the longest x3 78.4 us: conjugate_steps(): scaled = inverse * residual]
    psum x6 -> x0, blocking collectives: 112 us -> none  [the longest x3 94 us: global_pair(): return lax.psum((partial_pair[0], partial_pair[1]), 'gx')]
    ppermute x14 -> x0, starting transfers between devices: 34 us -> none  [the longest x6 23.7 us: with_halo(): lax.ppermute(tail, axis, [(i, (i + 1) % count) for i in range(ends)])]
    pallas_call x0 -> x1, Pallas kernels: none -> 32.2 us  [per_device(): pl.pallas_call(functools.partial(kernel, n_x, n_y), out_shape=(jax.ShapeD...]
    slice x37 -> x0, local copies, waits for them, and re-layouts: 26.9 us -> none  [the longest x30 24.5 us: element_energy(): weighted = weighted + stiffness[row_index, col_index] * views[col_index]]
    ppermute x14 -> x0, waiting for transfers between devices: 6.87 us -> none  [the longest x6 6.85 us: with_halo(): lax.ppermute(tail, axis, [(i, (i + 1) % count) for i in range(ends)])]
  transfers between devices with their start and end apart: 14 -> 0, of which waited for: 6 -> 0; matrix products, arithmetic and copies ran while one was open for 6% -> 0% of each run, Pallas kernels for 0% -> 0%
where the time goes in v1:
time: 37.3 us; the launch traced here: 37 us
  Pallas kernels  32.2 us (86%)
  local copies, waits for them, and re-layouts  4.19 us (11%)
  between operations  0.65 us (2%)
    pallas_call x1, Pallas kernels, per_device(): pl.pallas_call(functools.partial(kernel, n_x, n_y), out_shape=(jax.ShapeD...  32.2 us
    unnamed x8, local copies, waits for them, and re-layouts  4.19 us

profile of v1, /device:TPU:0, one launch (start us, length us, event | category | flops | bytes accessed | tf_op | source)
XLA Modules:
  0.0 37.0 jit_solution(3648815828994121198)
XLA Ops:
  0.6 0.0 copy-start
  0.6 1.1 %copy-done = f32[3,8,16,512]{3,2,1,0:T(8,128)S(1)} copy-done((f32[3,8,16,512]{3,2,1,0:T(8,128)S(1)}, f32[3,8,16,512]{3,2,1,0:T(8,128)}, u32[]{:S(2)}) %copy-start) | copy-done | bytes 786456
  1.8 0.0 copy-start.1
  1.8 0.9 %copy-done.1 = f32[8,16,512]{2,1,0:T(8,128)S(1)} copy-done((f32[8,16,512]{2,1,0:T(8,128)S(1)}, f32[8,16,512]{2,1,0:T(8,128)}, u32[]{:S(2)}) %copy-start.1) | copy-done | bytes 262168
  2.7 0.0 copy-start.2
  2.7 0.7 %copy-done.2 = f32[24,24]{1,0:T(8,128)S(1)} copy-done((f32[24,24]{1,0:T(8,128)S(1)}, f32[24,24]{1,0:T(8,128)}, u32[]{:S(2)}) %copy-start.2) | copy-done | bytes 2328
  3.4 32.2 %shard_map.50 = (f32[8,16,512]{2,1,0:T(8,128)S(1)}, f32[8,16,512]{2,1,0:T(8,128)S(1)}) custom-call(f32[3,8,16,512]{3,2,1,0:T(8,128)S(1)} %copy-done, f32[8,16,512]{2,1,0:T(8,128)S(1)} %copy-done.1, f32[24,24]{1,0:T(8,128)S(1)} %copy-done.2), custom_call_target="tpu_custom_call" | custom-call | tf_op jit(solution)/shard_map/pallas_call | solution.py:322
  35.6 0.7 %copy.7 = f32[8,16,512]{2,1,0:T(8,128)} copy(f32[8,16,512]{2,1,0:T(8,128)S(1)} %get-tuple-element.4) | data formatting | bytes 524288
  36.3 0.7 %copy.8 = f32[8,16,512]{2,1,0:T(8,128)} copy(f32[8,16,512]{2,1,0:T(8,128)S(1)} %get-tuple-element.5) | data formatting | bytes 524288
Async XLA Ops:
  0.6 1.1 %copy-start = (f32[3,8,16,512]{3,2,1,0:T(8,128)S(1)}, f32[3,8,16,512]{3,2,1,0:T(8,128)}, u32[]{:S(2)}) copy-start(f32[3,8,16,512]{3,2,1,0:T(8,128)} %disp.1) | copy-start | bytes 2359300
  1.8 0.9 %copy-start.1 = (f32[8,16,512]{2,1,0:T(8,128)S(1)}, f32[8,16,512]{2,1,0:T(8,128)}, u32[]{:S(2)}) copy-start(f32[8,16,512]{2,1,0:T(8,128)} %dens.1) | copy-start | bytes 786436
  2.7 0.7 %copy-start.2 = (f32[24,24]{1,0:T(8,128)S(1)}, f32[24,24]{1,0:T(8,128)}, u32[]{:S(2)}) copy-start(f32[24,24]{1,0:T(8,128)} %stiff.1) | copy-start | bytes 6916

commit v2 on v1

--- a/solution.py
+++ b/solution.py
@@ -15,8 +15,9 @@
 
 def kernel(
     n_x, n_y,
-    disp, dens, stiff,
-    sens, filt,
+    disp_in, dens_in, stiff_in,
+    sens_out, filt_out,
+    disp, dens, stiff, load_sems, sens, filt, store_sems,
     views, x_in, y_out, y_in, c_out, c_in,
     field0, field1, field2, image0, image1, image2, face_out, face_in, dots_out, dots_in,
     halo_send, halo_recv, face_send, face_recv, dots_send, dots_recv,
@@ -31,6 +32,13 @@
     def place(index):
         return {"gx": index // n_y, "gy": lax.rem(index, n_y)}
 
+    loads = [
+        pltpu.make_async_copy(disp_in, disp, load_sems.at[0]),
+        pltpu.make_async_copy(stiff_in, stiff, load_sems.at[1]),
+        pltpu.make_async_copy(dens_in, dens, load_sems.at[2]),
+    ]
+    for load in loads:
+        load.start()
     barrier = pltpu.get_barrier_semaphore()
 
     @pl.loop(1, count)
@@ -39,37 +47,38 @@
             barrier, inc=1, device_id=place(lax.rem(me + offset, count)), device_id_type=MESH
         )
 
+    @pl.when(jnp.logical_not(has_xn))
+    def _():
+        x_in[...] = jnp.zeros_like(x_in)
+        for field in (field0, field1, field2):
+            field[size_x + 1] = jnp.zeros((size_y, size_z), jnp.float32)
+
+    @pl.when(jnp.logical_not(has_xp))
+    def _():
+        for field in (field0, field1, field2):
+            field[0] = jnp.zeros((size_y, size_z), jnp.float32)
+
+    @pl.when(jnp.logical_not(has_yn))
+    def _():
+        y_in[...] = jnp.zeros_like(y_in)
+        for step in range(3):
+            face_in[step, 1] = jnp.zeros((size_x, size_z), jnp.float32)
+
+    @pl.when(jnp.logical_not(has_yp))
+    def _():
+        for step in range(3):
+            face_in[step, 0] = jnp.zeros((size_x, size_z), jnp.float32)
+
+    @pl.when(jnp.logical_not(jnp.logical_and(has_xn, has_yn)))
+    def _():
+        c_in[...] = jnp.zeros_like(c_in)
+
+    loads[0].wait()
     c_out[...] = jnp.zeros_like(c_out)
     for m in range(3):
         for i in range(size_x):
             y_out[m, i : i + 1, :] = disp[m, i, 0:1, :]
         c_out[m : m + 1, :] = disp[m, 0, 0:1, :]
-
-    @pl.when(jnp.logical_not(has_xn))
-    def _():
-        x_in[...] = jnp.zeros_like(x_in)
-        for field in (field0, field1, field2):
-            field[size_x + 1] = jnp.zeros((size_y, size_z), jnp.float32)
-
-    @pl.when(jnp.logical_not(has_xp))
-    def _():
-        for field in (field0, field1, field2):
-            field[0] = jnp.zeros((size_y, size_z), jnp.float32)
-
-    @pl.when(jnp.logical_not(has_yn))
-    def _():
-        y_in[...] = jnp.zeros_like(y_in)
-        for step in range(3):
-            face_in[step, 1] = jnp.zeros((size_x, size_z), jnp.float32)
-
-    @pl.when(jnp.logical_not(has_yp))
-    def _():
-        for step in range(3):
-            face_in[step, 0] = jnp.zeros((size_x, size_z), jnp.float32)
-
-    @pl.when(jnp.logical_not(jnp.logical_and(has_xn, has_yn)))
-    def _():
-        c_in[...] = jnp.zeros_like(c_in)
 
     pl.semaphore_wait(barrier, count - 1)
 
@@ -127,6 +136,9 @@
             energy = term if energy is None else energy + term
         rho = dens[i, start : start + 8, :]
         sens[i, start : start + 8, :] = (-2.0 * penal * (1.0 - e_min)) * (rho * rho) * energy
+
+    loads[1].wait()
+    loads[2].wait()
 
     @pl.loop(0, size_x - 1)
     def _(i):
@@ -184,13 +196,15 @@
                     face_recv.at[step, 3], me_x, me_y + 1), has_yn, has_yp),
         )
 
-    def exchange(step, field):
+    def start_exchange(step, field):
         copies = faces(step, field)
         for copy, sends, _ in copies:
             pl.when(sends)(copy.start)
+        return copies
+
+    def finish_exchange(copies):
         for copy, _, receives in copies:
             pl.when(receives)(copy.wait_recv)
-        return copies
 
     def apply(step, field, i):
         value = field[i + 1]
@@ -245,7 +259,10 @@
         put_field(0, field0, i, sens[i] / diagonal(i))
 
     zero = jnp.zeros((8, 128), jnp.float32)
-    sent = exchange(0, field0)
+    sent0 = start_exchange(0, field0)
+    store_sens = pltpu.make_async_copy(sens, sens_out, store_sems.at[0])
+    store_sens.start()
+    finish_exchange(sent0)
 
     def first(i, sums):
         image = apply(0, field0, i)
@@ -255,8 +272,9 @@
         return (sums[0] + fold(sens[i] * scaled), sums[1] + fold(image * scaled))
 
     dots = lax.fori_loop(0, size_x, first, (zero, zero))
+    sent1 = start_exchange(1, field1)
     send_dots(0, dots)
-    sent = sent + exchange(1, field1)
+    finish_exchange(sent1)
 
     @pl.loop(0, size_x)
     def _(i):
@@ -264,7 +282,8 @@
         image1[i] = image
         put_field(2, field2, i, image / diagonal(i))
 
-    sent = sent + exchange(2, field2)
+    sent2 = start_exchange(2, field2)
+    finish_exchange(sent2)
 
     @pl.loop(0, size_x)
     def _(i):
@@ -303,11 +322,15 @@
     def _(i):
         filt[i] = weight0 * field0[i + 1] + weight1 * field1[i + 1] + weight2 * field2[i + 1]
 
-    for copy, sends, _ in sent:
+    store_filt = pltpu.make_async_copy(filt, filt_out, store_sems.at[1])
+    store_filt.start()
+    for copy, sends, _ in sent0 + sent1 + sent2:
         pl.when(sends)(copy.wait_send)
     for which in range(2):
         whole = dots_in.at[which, pl.ds(0, count - 1)]
         pltpu.make_async_copy(whole, whole, dots_send.at[which]).wait()
+    store_sens.wait()
+    store_filt.wait()
 
 
 def solution(mesh):
@@ -318,13 +341,19 @@
         block = (size_x, size_y, size_z)
         wide = pltpu.VMEM((size_x + 2, size_y, size_z), jnp.float32)
         same = pltpu.VMEM(block, jnp.float32)
-        vmem = pl.BlockSpec(memory_space=pltpu.VMEM)
         return pl.pallas_call(
             functools.partial(kernel, n_x, n_y),
             out_shape=(jax.ShapeDtypeStruct(block, jnp.float32),) * 2,
-            in_specs=[vmem, vmem, pl.BlockSpec(memory_space=pltpu.SMEM)],
-            out_specs=(vmem, vmem),
+            in_specs=[pl.BlockSpec(memory_space=pltpu.HBM)] * 3,
+            out_specs=(pl.BlockSpec(memory_space=pltpu.HBM),) * 2,
             scratch_shapes=[
+                pltpu.VMEM(displacement.shape, jnp.float32),
+                same,
+                pltpu.SMEM(stiffness.shape, jnp.float32),
+                pltpu.SemaphoreType.DMA((3,)),
+                same,
+                same,
+                pltpu.SemaphoreType.DMA((2,)),
                 pltpu.VMEM((4, 3, size_x + 1, size_y, size_z), jnp.float32),
                 pltpu.VMEM((3, size_y, size_z), jnp.float32),
                 pltpu.VMEM((3, size_x, size_z), jnp.float32),
@@ -344,7 +373,7 @@
                 pltpu.SemaphoreType.DMA((2,)),
             ],
             compiler_params=pltpu.CompilerParams(
-                collective_id=0, has_side_effects=True, vmem_limit_bytes=48 * 1024 * 1024
+                collective_id=0, has_side_effects=True, vmem_limit_bytes=62 * 1024 * 1024
             ),
         )(displacement, density, stiffness)
 

time: 37.3 us -> 35 us (0.938)
  local copies, waits for them, and re-layouts: 4.19 us -> 2.42 us
  Pallas kernels: 32.2 us -> 31.8 us
    unnamed x8 -> x4, local copies, waits for them, and re-layouts: 4.19 us -> 2.42 us
    pallas_call x1, Pallas kernels: 32.2 us -> 31.8 us  [per_device(): pl.pallas_call(functools.partial(kernel, n_x, n_y), out_shape=(jax.ShapeD...]
where the time goes in v2:
time: 35 us; the launch traced here: 34.9 us
  Pallas kernels  31.8 us (91%)
  local copies, waits for them, and re-layouts  2.42 us (7%)
  between operations  0.65 us (2%)
    pallas_call x1, Pallas kernels, per_device(): pl.pallas_call(functools.partial(kernel, n_x, n_y), out_shape=(jax.ShapeD...  31.8 us
    unnamed x4, local copies, waits for them, and re-layouts  2.42 us

profile of v2, /device:TPU:0, one launch (start us, length us, event | category | flops | bytes accessed | tf_op | source)
XLA Modules:
  0.0 34.9 jit_solution(14989605787131436198)
XLA Ops:
  0.6 31.8 %shard_map.50 = (f32[8,16,512]{2,1,0:T(8,128)}, f32[8,16,512]{2,1,0:T(8,128)}) custom-call(f32[3,8,16,512]{3,2,1,0:T(8,128)} %disp_in.1, f32[8,16,512]{2,1,0:T(8,128)} %dens_in.1, f32[24,24]{1,0:T(8,128)} %stiff_in.1), custom_call_target="tpu_custom_call" | custom-call | tf_op jit(solution)/shard_map/pallas_call | solution.py:344
  32.4 0.0 copy-start
  32.4 1.7 %copy.7 = f32[8,16,512]{2,1,0:T(8,128)} copy(f32[8,16,512]{2,1,0:T(8,128)} %get-tuple-element.4) | data formatting | bytes 524288
  34.2 0.0 copy-done
  34.2 0.7 %copy.8 = f32[8,16,512]{2,1,0:T(8,128)} copy(f32[8,16,512]{2,1,0:T(8,128)S(1)} %copy-done) | data formatting | bytes 524288
Async XLA Ops:
  32.4 1.7 %copy-start = (f32[8,16,512]{2,1,0:T(8,128)S(1)}, f32[8,16,512]{2,1,0:T(8,128)}, u32[]{:S(2)}) copy-start(f32[8,16,512]{2,1,0:T(8,128)} %get-tuple-element.5) | copy-start | bytes 786436

commit v3 on v2

--- a/solution.py
+++ b/solution.py
@@ -117,7 +117,7 @@
         views[2, m, i] = upper
         views[3, m, i] = later_z(upper)
 
-    @pl.loop(0, size_x)
+    @pl.loop(0, size_x, unroll=True)
     def _(i):
         for m in range(3):
             put_views(m, i, disp[m, i], None)
@@ -149,7 +149,7 @@
     for m in range(3):
         put_views(m, size_x, x_in[m], c_in[m : m + 1, :])
 
-    @pl.loop(0, size_x)
+    @pl.loop(0, size_x, unroll=True)
     def _(i):
         for m in range(3):
             last = y_in[m, pl.ds(i, 1), :]
@@ -254,7 +254,7 @@
             for index in range(number)
         ]
 
-    @pl.loop(0, size_x)
+    @pl.loop(0, size_x, unroll=True)
     def _(i):
         put_field(0, field0, i, sens[i] / diagonal(i))
 
@@ -271,12 +271,12 @@
         scaled = field0[i + 1]
         return (sums[0] + fold(sens[i] * scaled), sums[1] + fold(image * scaled))
 
-    dots = lax.fori_loop(0, size_x, first, (zero, zero))
+    dots = lax.fori_loop(0, size_x, first, (zero, zero), unroll=True)
     sent1 = start_exchange(1, field1)
     send_dots(0, dots)
     finish_exchange(sent1)
 
-    @pl.loop(0, size_x)
+    @pl.loop(0, size_x, unroll=True)
     def _(i):
         image = apply(1, field1, i)
         image1[i] = image
@@ -285,7 +285,7 @@
     sent2 = start_exchange(2, field2)
     finish_exchange(sent2)
 
-    @pl.loop(0, size_x)
+    @pl.loop(0, size_x, unroll=True)
     def _(i):
         image2[i] = apply(2, field2, i)
 
@@ -302,7 +302,7 @@
         terms = (r1 * z1, z1 * az1, y1 * az1, az1 * w1, w1 * im0, y1 * ay1, y1 * im1, w1 * im1)
         return tuple(total + fold(term) for total, term in zip(sums, terms))
 
-    dots = lax.fori_loop(0, size_x, second, (zero,) * 8)
+    dots = lax.fori_loop(0, size_x, second, (zero,) * 8, unroll=True)
     send_dots(1, dots)
     g1, c1, d1, d2, d3, e1, e2, e3 = take_dots(1, 8)
     b1 = g1 / g0
@@ -318,7 +318,7 @@
     weight1 = -(s1 * s0 + s2 * (t1 + b2 * s0))
     weight2 = s2 * s0 * s1
 
-    @pl.loop(0, size_x)
+    @pl.loop(0, size_x, unroll=True)
     def _(i):
         filt[i] = weight0 * field0[i + 1] + weight1 * field1[i + 1] + weight2 * field2[i + 1]
 

time: 35 us -> 32.4 us (0.926)
  Pallas kernels: 31.8 us -> 29.2 us
    pallas_call x1, Pallas kernels: 31.8 us -> 29.2 us  [per_device(): pl.pallas_call(functools.partial(kernel, n_x, n_y), out_shape=(jax.ShapeD...]
where the time goes in v3:
time: 32.4 us; the launch traced here: 32.2 us
  Pallas kernels  29.2 us (90%)
  local copies, waits for them, and re-layouts  2.42 us (7%)
  between operations  0.65 us (2%)
    pallas_call x1, Pallas kernels, per_device(): pl.pallas_call(functools.partial(kernel, n_x, n_y), out_shape=(jax.ShapeD...  29.2 us
    unnamed x4, local copies, waits for them, and re-layouts  2.42 us

profile of v3, /device:TPU:0, one launch (start us, length us, event | category | flops | bytes accessed | tf_op | source)
XLA Modules:
  0.0 32.2 jit_solution(18295074758967557422)
XLA Ops:
  0.6 29.2 %shard_map.50 = (f32[8,16,512]{2,1,0:T(8,128)}, f32[8,16,512]{2,1,0:T(8,128)}) custom-call(f32[3,8,16,512]{3,2,1,0:T(8,128)} %disp_in.1, f32[8,16,512]{2,1,0:T(8,128)} %dens_in.1, f32[24,24]{1,0:T(8,128)} %stiff_in.1), custom_call_target="tpu_custom_call" | custom-call | tf_op jit(solution)/shard_map/pallas_call | solution.py:344
  29.8 0.0 copy-start
  29.8 1.7 %copy.7 = f32[8,16,512]{2,1,0:T(8,128)} copy(f32[8,16,512]{2,1,0:T(8,128)} %get-tuple-element.4) | data formatting | bytes 524288
  31.5 0.0 copy-done
  31.5 0.7 %copy.8 = f32[8,16,512]{2,1,0:T(8,128)} copy(f32[8,16,512]{2,1,0:T(8,128)S(1)} %copy-done) | data formatting | bytes 524288
Async XLA Ops:
  29.8 1.7 %copy-start = (f32[8,16,512]{2,1,0:T(8,128)S(1)}, f32[8,16,512]{2,1,0:T(8,128)}, u32[]{:S(2)}) copy-start(f32[8,16,512]{2,1,0:T(8,128)} %get-tuple-element.5) | copy-start | bytes 786436

commit v4 on v3

--- a/solution.py
+++ b/solution.py
@@ -41,7 +41,7 @@
         load.start()
     barrier = pltpu.get_barrier_semaphore()
 
-    @pl.loop(1, count)
+    @pl.loop(1, count, unroll=4)
     def _(offset):
         pl.semaphore_signal(
             barrier, inc=1, device_id=place(lax.rem(me + offset, count)), device_id_type=MESH
@@ -74,12 +74,6 @@
         c_in[...] = jnp.zeros_like(c_in)
 
     loads[0].wait()
-    c_out[...] = jnp.zeros_like(c_out)
-    for m in range(3):
-        for i in range(size_x):
-            y_out[m, i : i + 1, :] = disp[m, i, 0:1, :]
-        c_out[m : m + 1, :] = disp[m, 0, 0:1, :]
-
     pl.semaphore_wait(barrier, count - 1)
 
     def remote(src, dst, send, recv, to_x, to_y):
@@ -96,7 +90,14 @@
         (halo_y, has_yp, has_yn),
         (halo_c, jnp.logical_and(has_xp, has_yp), jnp.logical_and(has_xn, has_yn)),
     )
-    for copy, sends, _ in halos:
+    pl.when(has_xp)(halo_x.start)
+    c_out[...] = jnp.zeros_like(c_out)
+    for m in range(3):
+        for i in range(size_x):
+            y_out[m, i : i + 1, :] = disp[m, i, 0:1, :]
+        c_out[m : m + 1, :] = disp[m, 0, 0:1, :]
+
+    for copy, sends, _ in halos[1:]:
         pl.when(sends)(copy.start)
 
     rows = lax.broadcasted_iota(jnp.int32, (size_y, size_z), 0)
@@ -239,7 +240,7 @@
         dots_out[which] = row
         dots_in[which, count - 1] = row
 
-        @pl.loop(1, count)
+        @pl.loop(1, count, unroll=4)
         def _(offset):
             to = place(lax.rem(me + offset, count))
             remote(dots_out.at[which], dots_in.at[which, offset - 1], dots_send.at[which],
@@ -318,19 +319,24 @@
     weight1 = -(s1 * s0 + s2 * (t1 + b2 * s0))
     weight2 = s2 * s0 * s1
 
-    @pl.loop(0, size_x, unroll=True)
-    def _(i):
-        filt[i] = weight0 * field0[i + 1] + weight1 * field1[i + 1] + weight2 * field2[i + 1]
-
-    store_filt = pltpu.make_async_copy(filt, filt_out, store_sems.at[1])
-    store_filt.start()
+    half = size_x // 2
+    store_filt = []
+    for part in range(2):
+        span = pl.ds(part * half, half)
+        for i in range(part * half, part * half + half):
+            filt[i] = weight0 * field0[i + 1] + weight1 * field1[i + 1] + weight2 * field2[i + 1]
+        store_filt.append(
+            pltpu.make_async_copy(filt.at[span], filt_out.at[span], store_sems.at[1 + part])
+        )
+        store_filt[part].start()
     for copy, sends, _ in sent0 + sent1 + sent2:
         pl.when(sends)(copy.wait_send)
     for which in range(2):
         whole = dots_in.at[which, pl.ds(0, count - 1)]
         pltpu.make_async_copy(whole, whole, dots_send.at[which]).wait()
     store_sens.wait()
-    store_filt.wait()
+    for store in store_filt:
+        store.wait()
 
 
 def solution(mesh):
@@ -353,7 +359,7 @@
                 pltpu.SemaphoreType.DMA((3,)),
                 same,
                 same,
-                pltpu.SemaphoreType.DMA((2,)),
+                pltpu.SemaphoreType.DMA((3,)),
                 pltpu.VMEM((4, 3, size_x + 1, size_y, size_z), jnp.float32),
                 pltpu.VMEM((3, size_y, size_z), jnp.float32),
                 pltpu.VMEM((3, size_x, size_z), jnp.float32),

time: 32.4 us -> 32.2 us (level)
  no operation moved by 1% of the time
where the time goes in v4:
time: 32.2 us; the launch traced here: 32 us
  Pallas kernels  29 us (90%)
  local copies, waits for them, and re-layouts  2.42 us (8%)
  between operations  0.65 us (2%)
    pallas_call x1, Pallas kernels, per_device(): pl.pallas_call(functools.partial(kernel, n_x, n_y), out_shape=(jax.ShapeD...  29 us
    unnamed x4, local copies, waits for them, and re-layouts  2.42 us

profile of v4, /device:TPU:0, one launch (start us, length us, event | category | flops | bytes accessed | tf_op | source)
XLA Modules:
  0.0 32.0 jit_solution(15187780204840044086)
XLA Ops:
  0.6 29.0 %shard_map.50 = (f32[8,16,512]{2,1,0:T(8,128)}, f32[8,16,512]{2,1,0:T(8,128)}) custom-call(f32[3,8,16,512]{3,2,1,0:T(8,128)} %disp_in.1, f32[8,16,512]{2,1,0:T(8,128)} %dens_in.1, f32[24,24]{1,0:T(8,128)} %stiff_in.1), custom_call_target="tpu_custom_call" | custom-call | tf_op jit(solution)/shard_map/pallas_call | solution.py:350
  29.6 0.0 copy-start
  29.6 1.7 %copy.7 = f32[8,16,512]{2,1,0:T(8,128)} copy(f32[8,16,512]{2,1,0:T(8,128)} %get-tuple-element.4) | data formatting | bytes 524288
  31.3 0.0 copy-done
  31.3 0.7 %copy.8 = f32[8,16,512]{2,1,0:T(8,128)} copy(f32[8,16,512]{2,1,0:T(8,128)S(1)} %copy-done) | data formatting | bytes 524288
Async XLA Ops:
  29.6 1.7 %copy-start = (f32[8,16,512]{2,1,0:T(8,128)S(1)}, f32[8,16,512]{2,1,0:T(8,128)}, u32[]{:S(2)}) copy-start(f32[8,16,512]{2,1,0:T(8,128)} %get-tuple-element.5) | copy-start | bytes 786436

commit v5 on v4

--- a/solution.py
+++ b/solution.py
@@ -41,7 +41,7 @@
         load.start()
     barrier = pltpu.get_barrier_semaphore()
 
-    @pl.loop(1, count, unroll=4)
+    @pl.loop(1, count, unroll=8)
     def _(offset):
         pl.semaphore_signal(
             barrier, inc=1, device_id=place(lax.rem(me + offset, count)), device_id_type=MESH
@@ -240,7 +240,7 @@
         dots_out[which] = row
         dots_in[which, count - 1] = row
 
-        @pl.loop(1, count, unroll=4)
+        @pl.loop(1, count, unroll=8)
         def _(offset):
             to = place(lax.rem(me + offset, count))
             remote(dots_out.at[which], dots_in.at[which, offset - 1], dots_send.at[which],

time: 32.2 us -> 32.2 us (level)
  no operation moved by 1% of the time
where the time goes in v5:
time: 32.2 us; the launch traced here: 32 us
  Pallas kernels  29 us (90%)
  local copies, waits for them, and re-layouts  2.42 us (8%)
  between operations  0.65 us (2%)
    pallas_call x1, Pallas kernels, per_device(): pl.pallas_call(functools.partial(kernel, n_x, n_y), out_shape=(jax.ShapeD...  29 us
    unnamed x4, local copies, waits for them, and re-layouts  2.42 us

profile of v5, /device:TPU:0, one launch (start us, length us, event | category | flops | bytes accessed | tf_op | source)
XLA Modules:
  0.0 32.0 jit_solution(12576462473498103586)
XLA Ops:
  0.6 29.0 %shard_map.50 = (f32[8,16,512]{2,1,0:T(8,128)}, f32[8,16,512]{2,1,0:T(8,128)}) custom-call(f32[3,8,16,512]{3,2,1,0:T(8,128)} %disp_in.1, f32[8,16,512]{2,1,0:T(8,128)} %dens_in.1, f32[24,24]{1,0:T(8,128)} %stiff_in.1), custom_call_target="tpu_custom_call" | custom-call | tf_op jit(solution)/shard_map/pallas_call | solution.py:350
  29.6 0.0 copy-start
  29.6 1.7 %copy.7 = f32[8,16,512]{2,1,0:T(8,128)} copy(f32[8,16,512]{2,1,0:T(8,128)} %get-tuple-element.4) | data formatting | bytes 524288
  31.3 0.0 copy-done
  31.3 0.7 %copy.8 = f32[8,16,512]{2,1,0:T(8,128)} copy(f32[8,16,512]{2,1,0:T(8,128)S(1)} %copy-done) | data formatting | bytes 524288
Async XLA Ops:
  29.6 1.7 %copy-start = (f32[8,16,512]{2,1,0:T(8,128)S(1)}, f32[8,16,512]{2,1,0:T(8,128)}, u32[]{:S(2)}) copy-start(f32[8,16,512]{2,1,0:T(8,128)} %get-tuple-element.5) | copy-start | bytes 786436
